TPU v7x, 32 devices: a whole 2x2x4 slice. The times are simulated.
32 devices in a mesh: dp: 8 (over z, y), seq: 4 (over x, core).
Axes of the slice: x: 2, y: 2, z: 4, core: 2. Of those that a mesh axis runs over, the one named last changes fastest.
Arguments:
- tokens: bfloat16 [8192, 768], P(('dp', 'seq')), may hold values from -6 to 6
- ln1_gain: bfloat16 [768], P('dp'), may hold values from 0.25 to 1.75
- w_qkv: bfloat16 [768, 2304], P('dp'), may hold values from -0.21875 to 0.21875
- w_out: bfloat16 [768, 768], P('dp'), may hold values from -1.75 to 1.75
- w_ada: bfloat16 [768, 2304], P('dp'), may hold values from -0.21875 to 0.21875
- w_up: bfloat16 [768, 3072], P('dp'), may hold values from -0.21875 to 0.21875
- w_down: bfloat16 [3072, 768], P('dp'), may hold values from -0.109375 to 0.109375
- out_grad: bfloat16 [8192, 768], P(('dp', 'seq')), may hold values from -6 to 6
- layout: int32 [8, 2], P('dp'), may hold values from 256 to 896, as said below
- timestep: int32 [8], P('dp'), may hold values from 0 to 999
Outputs:
- layer_out: bfloat16 [8192, 768], P(('dp', 'seq'))
- input_grad: bfloat16 [8192, 768], P(('dp', 'seq'))
- gain_grad: float32 [768], P('dp')
- qkv_weight_grad: float32 [768, 2304], P('dp')
- out_weight_grad: float32 [768, 768], P('dp')
- ada_weight_grad: float32 [768, 2304], P('dp')
- up_weight_grad: float32 [768, 3072], P('dp')
- down_weight_grad: float32 [3072, 768], P('dp')
Inputs may be any that keep to these rules, and one draw needn't show every extreme that they name: layout[g] = (P, C): tokens below P are the prompt, the first continuation runs from P to C - 1, the second from C to 1023; P lies between 256 and 512, and each continuation holds at least a quarter of the tokens after the prompt.
All inputs are finite; a program needn't handle non-finite values.
Results may differ from a plain program's by a relative error of at most 0.017.
Values may be sent and summed in bfloat16 or wider, within the bound.
No kernel may reach another device: no remote copies, remote signals or barrier semaphores. Data moves between devices by JAX's collectives and lax.ppermute only.
A program may use at most 128 MiB of HBM per device.

v0:
```python
import math
import jax
import jax.numpy as jnp
from jax import lax
from jax.sharding import PartitionSpec as P

HEADS = 12
HEAD_DIM = 64
eps = 1e-05
neg_fill = -1e30


def layer_norm(values_in):
    average = jnp.mean(values_in, axis=-1, keepdims=True)
    centred = values_in - average
    variance = jnp.mean(centred * centred, axis=-1, keepdims=True)
    scaling = lax.rsqrt(variance + eps)
    return (centred * scaling, scaling)


def norm_back(grad_normed, normed, scaling):
    first_mean = jnp.mean(grad_normed, axis=-1, keepdims=True)
    second_mean = jnp.mean(grad_normed * normed, axis=-1, keepdims=True)
    return scaling * (grad_normed - first_mean - normed * second_mean)


def rope_tables(positions):
    half_dim = HEAD_DIM // 2
    frequency = jnp.exp(
        -math.log(10000.0) * 2.0 * jnp.arange(half_dim, dtype=jnp.float32) / HEAD_DIM
    )
    angles = positions.astype(jnp.float32)[:, None] * frequency[None, :]
    return (jnp.cos(angles), jnp.sin(angles))


def rotate(values_in, cos_table, sine_table, direction):
    half_dim = HEAD_DIM // 2
    front_half = values_in[..., :half_dim]
    back_half = values_in[..., half_dim:]
    cos_part = cos_table[:, None, :]
    sine_part = sine_table[:, None, :] * direction
    return jnp.concatenate(
        [
            front_half * cos_part - back_half * sine_part,
            back_half * cos_part + front_half * sine_part,
        ],
        axis=-1,
    )


def visible(query_pos, key_pos, prompt_end, second_start):
    query_segment = (query_pos >= prompt_end).astype(jnp.int32) + (
        query_pos >= second_start
    ).astype(jnp.int32)
    key_segment = (key_pos >= prompt_end).astype(jnp.int32) + (key_pos >= second_start).astype(
        jnp.int32
    )
    return (key_pos[None, :] < prompt_end) | (query_segment[:, None] == key_segment[None, :])


def time_table(time_steps, model_width):
    half_dim = model_width // 2
    frequency = jnp.exp(-math.log(10000.0) * jnp.arange(half_dim, dtype=jnp.float32) / half_dim)
    angles = time_steps[:, None] * frequency[None, :]
    return jnp.concatenate([jnp.cos(angles), jnp.sin(angles)], axis=1)


def left_product(left, right):
    return lax.dot_general(
        left, right, (((0,), (0,)), ((), ())), preferred_element_type=jnp.float32
    )


def right_product(left, right):
    return lax.dot_general(
        left, right, (((1,), (1,)), ((), ())), preferred_element_type=jnp.float32
    )


def split_rows(grad_full, data_count):
    return grad_full.reshape(data_count, grad_full.shape[0] // data_count, -1)


def body(tokens, ln1_gain, w_qkv, w_out, w_ada, w_up, w_down, out_grad, layout, timestep):
    seq_count = lax.axis_size("seq")
    seq_rank = lax.axis_index("seq")
    tok_rows = tokens.shape[0]
    model_width = tokens.shape[1]
    group_rows = tok_rows * seq_count
    heads_local = HEADS // seq_count
    local_width = heads_local * HEAD_DIM
    block_rows = min(512, group_rows)
    blocks = group_rows // block_rows
    gain_full, qkv_weight, out_weight = (
        lax.all_gather(ln1_gain, "dp", axis=0, tiled=True),
        lax.all_gather(w_qkv, "dp", axis=0, tiled=True),
        lax.all_gather(w_out, "dp", axis=0, tiled=True),
    )
    ada_weight, up_weight, down_weight = (
        lax.all_gather(w_ada, "dp", axis=0, tiled=True),
        lax.all_gather(w_up, "dp", axis=0, tiled=True),
        lax.all_gather(w_down, "dp", axis=0, tiled=True),
    )
    gain_float = gain_full.astype(jnp.float32)
    inputs = tokens.astype(jnp.float32)
    normed_one, scaling_one = layer_norm(inputs)
    hidden_one = (normed_one * gain_float).astype(jnp.bfloat16)
    projected = jnp.dot(hidden_one, qkv_weight, preferred_element_type=jnp.float32).reshape(
        tok_rows, 3, HEADS, HEAD_DIM
    )
    positions = seq_rank * tok_rows + jnp.arange(tok_rows, dtype=jnp.int32)
    cos_table, sine_table = rope_tables(positions)
    rotated = jnp.stack(
        [
            rotate(projected[:, 0], cos_table, sine_table, 1.0),
            rotate(projected[:, 1], cos_table, sine_table, 1.0),
            projected[:, 2],
        ],
        axis=1,
    )
    outgoing = rotated.astype(jnp.bfloat16).reshape(tok_rows, 3, seq_count, local_width)
    incoming = lax.all_to_all(outgoing, "seq", split_axis=2, concat_axis=0, tiled=True).reshape(
        group_rows, 3, heads_local, HEAD_DIM
    )
    queries = incoming[:, 0]
    keys_all = incoming[:, 1]
    values_all = incoming[:, 2]
    prompt_end = layout[0, 0]
    second_start = layout[0, 1]
    key_pos = jnp.arange(group_rows, dtype=jnp.int32)

    def scores_of(query_block, start):
        raw_scores = (
            jnp.einsum("qhd,khd->hqk", query_block, keys_all, preferred_element_type=jnp.float32)
            * 0.125
        )
        query_pos = start + jnp.arange(block_rows, dtype=jnp.int32)
        allowed = visible(query_pos, key_pos, prompt_end, second_start)
        return jnp.where(allowed[None], raw_scores, neg_fill)

    query_blocks = queries.reshape(blocks, block_rows, heads_local, HEAD_DIM)
    starts = jnp.arange(blocks, dtype=jnp.int32) * block_rows

    def forward_block(operands):
        query_block, start = operands
        scores = scores_of(query_block, start)
        row_max = jnp.max(scores, axis=-1, keepdims=True)
        exponent = jnp.exp(scores - row_max)
        row_sum = jnp.sum(exponent, axis=-1, keepdims=True)
        attn_probs = (exponent / row_sum).astype(jnp.bfloat16)
        block_out = jnp.einsum(
            "hqk,khd->qhd", attn_probs, values_all, preferred_element_type=jnp.float32
        )
        return (block_out.astype(jnp.bfloat16), (row_max + jnp.log(row_sum))[..., 0])

    attended_heads, log_sums = lax.map(forward_block, (query_blocks, starts))
    attended = lax.all_to_all(
        attended_heads.reshape(group_rows, local_width),
        "seq",
        split_axis=0,
        concat_axis=1,
        tiled=True,
    )
    middle = inputs + jnp.dot(attended, out_weight, preferred_element_type=jnp.float32)
    time_embed = time_table(timestep.astype(jnp.float32), model_width).astype(jnp.bfloat16)
    modulation = jnp.dot(time_embed, ada_weight, preferred_element_type=jnp.float32)[0]
    mod_scale = modulation[:model_width]
    mod_shift = modulation[model_width : 2 * model_width]
    mod_gate = modulation[2 * model_width :]
    normed_two, scaling_two = layer_norm(middle)
    hidden_two = (normed_two * (1.0 + mod_scale) + mod_shift).astype(jnp.bfloat16)
    pre_act = jnp.dot(hidden_two, up_weight, preferred_element_type=jnp.float32)
    gelu_vals, gelu_pull = jax.vjp(lambda inner: jax.nn.gelu(inner, approximate=True), pre_act)
    activated = gelu_vals.astype(jnp.bfloat16)
    mlp_out = jnp.dot(activated, down_weight, preferred_element_type=jnp.float32)
    result = middle + mod_gate * mlp_out
    grad_out = out_grad.astype(jnp.float32)
    grad_mlp = (mod_gate * grad_out).astype(jnp.bfloat16)
    grad_gate = jnp.sum(grad_out * mlp_out, axis=0)
    grad_wdown = left_product(activated, grad_mlp)
    grad_act = right_product(grad_mlp, down_weight)
    grad_pre = gelu_pull(grad_act)[0].astype(jnp.bfloat16)
    grad_wup = left_product(hidden_two, grad_pre)
    grad_hidden_two = right_product(grad_pre, up_weight)
    grad_scale = jnp.sum(grad_hidden_two * normed_two, axis=0)
    grad_shift = jnp.sum(grad_hidden_two, axis=0)
    grad_middle = grad_out + norm_back(grad_hidden_two * (1.0 + mod_scale), normed_two, scaling_two)
    grad_mod = jnp.concatenate([grad_scale, grad_shift, grad_gate])
    grad_branch = grad_middle.astype(jnp.bfloat16)
    grad_wout = left_product(attended, grad_branch)
    grad_attn = right_product(grad_branch, out_weight).astype(jnp.bfloat16)
    grad_heads = lax.all_to_all(grad_attn, "seq", split_axis=1, concat_axis=0, tiled=True).reshape(
        blocks, block_rows, heads_local, HEAD_DIM
    )

    def backward_block(carry, operands):
        key_grad, value_grad = carry
        query_block, start, grad_block, lse_block = operands
        scores = scores_of(query_block, start)
        attn_probs = jnp.exp(scores - lse_block[..., None])
        value_grad = value_grad + jnp.einsum(
            "hqk,qhd->khd",
            attn_probs.astype(jnp.bfloat16),
            grad_block,
            preferred_element_type=jnp.float32,
        )
        prob_grad = jnp.einsum(
            "qhd,khd->hqk", grad_block, values_all, preferred_element_type=jnp.float32
        )
        row_centre = jnp.sum(attn_probs * prob_grad, axis=-1, keepdims=True)
        score_grad = (attn_probs * (prob_grad - row_centre)).astype(jnp.bfloat16)
        query_grad = (
            jnp.einsum("hqk,khd->qhd", score_grad, keys_all, preferred_element_type=jnp.float32)
            * 0.125
        )
        key_grad = (
            key_grad
            + jnp.einsum(
                "hqk,qhd->khd", score_grad, query_block, preferred_element_type=jnp.float32
            )
            * 0.125
        )
        return ((key_grad, value_grad), query_grad)

    zero_grad = jnp.zeros((group_rows, heads_local, HEAD_DIM), jnp.float32)
    (key_grad, value_grad), query_grads = lax.scan(
        backward_block, (zero_grad, zero_grad), (query_blocks, starts, grad_heads, log_sums)
    )
    stacked = jnp.stack(
        [query_grads.reshape(group_rows, heads_local, HEAD_DIM), key_grad, value_grad], axis=1
    )
    stacked = stacked.astype(jnp.bfloat16).reshape(group_rows, 3, 1, local_width)
    returned = (
        lax.all_to_all(stacked, "seq", split_axis=0, concat_axis=2, tiled=True)
        .astype(jnp.float32)
        .reshape(tok_rows, 3, HEADS, HEAD_DIM)
    )
    grad_qkv = jnp.stack(
        [
            rotate(returned[:, 0], cos_table, sine_table, -1.0),
            rotate(returned[:, 1], cos_table, sine_table, -1.0),
            returned[:, 2],
        ],
        axis=1,
    )
    grad_qkv = grad_qkv.reshape(tok_rows, 3 * model_width).astype(jnp.bfloat16)
    grad_wqkv = left_product(hidden_one, grad_qkv)
    grad_hidden_one = right_product(grad_qkv, qkv_weight)
    grad_gain = jnp.sum(grad_hidden_one * normed_one, axis=0)
    grad_inputs = grad_middle + norm_back(grad_hidden_one * gain_float, normed_one, scaling_one)
    qkv_cols = 3 * model_width
    grad_wada = time_embed.astype(jnp.float32).reshape(-1)[:, None] * grad_mod[None, :]
    grad_joint = jnp.concatenate([grad_wqkv, grad_wada], axis=1)
    data_count = lax.axis_size("dp")
    parts = (
        lax.psum_scatter(
            split_rows(grad_gain, data_count).astype(jnp.bfloat16),
            "seq",
            scatter_dimension=1,
            tiled=True,
        ).astype(jnp.float32),
        lax.psum_scatter(
            split_rows(grad_joint, data_count).astype(jnp.bfloat16),
            "seq",
            scatter_dimension=1,
            tiled=True,
        ).astype(jnp.float32),
        lax.psum_scatter(
            split_rows(grad_wout, data_count).astype(jnp.bfloat16),
            "seq",
            scatter_dimension=1,
            tiled=True,
        ).astype(jnp.float32),
        lax.psum_scatter(
            split_rows(grad_wup, data_count).astype(jnp.bfloat16),
            "seq",
            scatter_dimension=1,
            tiled=True,
        ).astype(jnp.float32),
        lax.psum_scatter(
            split_rows(grad_wdown, data_count).astype(jnp.bfloat16),
            "seq",
            scatter_dimension=1,
            tiled=True,
        ).astype(jnp.float32),
    )
    owned = (
        lax.psum_scatter(parts[0], "dp", scatter_dimension=0, tiled=True),
        lax.psum_scatter(parts[1], "dp", scatter_dimension=0, tiled=True),
        lax.psum_scatter(parts[2], "dp", scatter_dimension=0, tiled=True),
        lax.psum_scatter(parts[3], "dp", scatter_dimension=0, tiled=True),
        lax.psum_scatter(parts[4], "dp", scatter_dimension=0, tiled=True),
    )
    spread = (
        lax.all_gather(owned[0].astype(jnp.bfloat16), "seq", axis=1, tiled=True).astype(
            jnp.float32
        ),
        lax.all_gather(owned[1].astype(jnp.bfloat16), "seq", axis=1, tiled=True).astype(
            jnp.float32
        ),
        lax.all_gather(owned[2].astype(jnp.bfloat16), "seq", axis=1, tiled=True).astype(
            jnp.float32
        ),
        lax.all_gather(owned[3].astype(jnp.bfloat16), "seq", axis=1, tiled=True).astype(
            jnp.float32
        ),
        lax.all_gather(owned[4].astype(jnp.bfloat16), "seq", axis=1, tiled=True).astype(
            jnp.float32
        ),
    )
    final_gain = spread[0].reshape(-1)
    final_joint = spread[1].reshape(spread[1].shape[1], -1)
    final_out = spread[2].reshape(spread[2].shape[1], -1)
    final_up = spread[3].reshape(spread[3].shape[1], -1)
    final_down = spread[4].reshape(spread[4].shape[1], -1)
    final_qkv = final_joint[:, :qkv_cols]
    final_ada = final_joint[:, qkv_cols:]
    return (
        result.astype(jnp.bfloat16),
        grad_inputs.astype(jnp.bfloat16),
        final_gain,
        final_qkv,
        final_out,
        final_ada,
        final_up,
        final_down,
    )


def solution(mesh):
    placed = (
        P(("dp", "seq"), None),
        P("dp"),
        P("dp", None),
        P("dp", None),
        P("dp", None),
        P("dp", None),
        P("dp", None),
        P(("dp", "seq"), None),
        P("dp", None),
        P("dp"),
    )
    return jax.shard_map(
        body,
        mesh=mesh,
        in_specs=placed,
        out_specs=(
            P(("dp", "seq"), None),
            P(("dp", "seq"), None),
            P("dp"),
            P("dp", None),
            P("dp", None),
            P("dp", None),
            P("dp", None),
            P("dp", None),
        ),
        check_vma=False,
    )
```

profile of v0, /device:TPU:0, one launch (start us, length us, event | category | flops | bytes accessed | tf_op | source)
XLA Modules:
  0.0 863.8 jit_solution(9710499089409813553)
XLA Ops:
  12.9 23.2 %all-reduce = bf16[768]{0:T(1024)(128)(2,1)S(1)} all-reduce(bf16[768]{0:T(1024)(128)(2,1)S(1)} %dynamic-update-slice), channel_id=1, replica_groups=mesh['dp'=8,'seq'=4] {'dp'}, use_global_device_ids=true, to_apply=%add | all-reduce | flops 768 | bytes 3072
  39.3 39.0 %all-gather.6.cloned.1.call-done = bf16[768,2304]{1,0:T(8,128)(2,1)} async-done(((bf16[96,2304]{1,0:T(8,128)(2,1)}), bf16[768,2304]{1,0:T(8,128)(2,1)}) %all-gather.6.cloned.1.call-update) | async-done | bytes 3538960 | tf_op jit(solution)/shard_map/all_gather | solution.py:96
  78.3 3.7 fusion.85
  83.8 3.5 all-to-all-start
  89.9 13.3 %all-to-all-done = bf16[256,3,4,192]{0,3,1,2:T(8,128)(2,1)S(1)} async-done(((bf16[256,3,4,192]{0,3,1,2:T(8,128)(2,1)}), bf16[256,3,4,192]{0,3,1,2:T(8,128)(2,1)S(1)}, u32[]{:S(2)}, u32[]{:S(2)}) %all-to-all-start) | async-done | bytes 1179680 | tf_op jit(solution)/shard_map/all_to_all | solution.py:122
  106.9 25.5 %while.30 = (s32[]{:T(128)}, bf16[2,512,3,64]{1,3,2,0:T(8,128)(2,1)S(1)}, f32[2,3,512]{2,1,0:T(4,128)}, s32[]{:T(128)}, s32[2]{0:T(128)S(1)}, /*index=5*/s32[]{:...) while((s32[]{:T(128)}, ...), condition=%wide.region_5.6_spmd.clone.clone, body=%wide.region_2.5_spmd.clone.clone.sunk | while | flops 422682112 | bytes 22220956 | solution.py:156
  115.8 3.2 fusion.143
  128.6 3.2 fusion.143
  133.8 3.5 all-to-all-start.1
  137.8 6.4 all-gather.10.cloned.1.call-done
  144.2 2.6 convolution_reduce_fusion
  146.8 39.1 %all-gather.8.cloned.1.call-done = bf16[768,768]{1,0:T(8,128)(2,1)} async-done(((bf16[96,768]{1,0:T(8,128)(2,1)}), bf16[768,768]{1,0:T(8,128)(2,1)}) %all-gather.8.cloned.1.call-update) | async-done | bytes 1179664 | tf_op jit(solution)/shard_map/all_gather | solution.py:97
  188.1 78.6 %all-gather.12.cloned.1.call-done = bf16[768,3072]{1,0:T(8,128)(2,1)} async-done(((bf16[96,3072]{1,0:T(8,128)(2,1)}), bf16[768,3072]{1,0:T(8,128)(2,1)}) %all-gather.12.cloned.1.call-update) | async-done | bytes 4718608 | tf_op jit(solution)/shard_map/all_gather | solution.py:101
  266.7 5.5 fusion.87
  272.2 74.6 %all-gather.14.cloned.1.call-done = bf16[3072,768]{1,0:T(8,128)(2,1)} async-done(((bf16[384,768]{1,0:T(8,128)(2,1)}), bf16[3072,768]{1,0:T(8,128)(2,1)}) %all-gather.14.cloned.1.call-update) | async-done | bytes 4718608 | tf_op jit(solution)/shard_map/all_gather | solution.py:102
  346.8 6.7 fusion.56
  357.4 3.5 fusion.72
  362.6 6.4 convolution_convert_fusion
  371.7 3.5 all-to-all-start.2
  375.4 3.0 convolution_convert_fusion.1
  378.4 2.6 copy.99
  381.0 5.4 all-to-all-done.2
  387.8 45.0 %while.31 = (s32[]{:T(128)}, f32[1024,3,64]{0,2,1:T(8,128)}, f32[1024,3,64]{0,2,1:T(8,128)}, bf16[2,512,3,64]{1,3,2,0:T(8,128)(2,1)}, bf16[2,512,3,64]{1,3,2,0:T...) while((s32[]{:T(128)}, f32[1024,3,64]{0,2,1:T(8,128)}, ...), condition=%wide.region_12.13_spmd.clone.clone, body=%wide.region_10.12_spmd.clone.clone.sunk | while | flops 1032363520 | bytes 110420320 | solution.py:226
  395.2 3.8 multiply_reduce_fusion.7
  400.9 2.7 fusion.154
  404.2 4.0 fusion.155
  417.5 3.8 multiply_reduce_fusion.7
  423.1 2.9 fusion.154
  426.6 4.3 fusion.155
  437.0 2.5 copy.80
  439.5 3.6 all-to-all-start.3
  445.6 30.9 %all-to-all-done.3 = bf16[1024,3,1,192]{3,1,2,0:T(4,128)(2,1)S(1)} async-done(((bf16[1024,3,1,192]{3,1,2,0:T(4,128)(2,1)}), bf16[1024,3,1,192]{3,1,2,0:T(4,128)(2,1)S(1)}, u32[]{:S(2)}, u32[]{:S(2)}) %all-to-all-start.3) | async-done | bytes 1179680 | tf_op jit(solution)/shard_map/all_to_all | solution.py:234
  476.5 2.8 copy.84
  482.6 5.5 pad_maximum_fusion
  488.0 6.7 copy.95
  501.7 56.8 %reduce-scatter.27.cloned.1.call-done = bf16[24,36864]{1,0:T(8,128)(2,1)} async-done(((bf16[96,36864]{1,0:T(8,128)(2,1)}), bf16[24,36864]{1,0:T(8,128)(2,1)}) %reduce-scatter.27.cloned.1.call-update) | async-done | bytes 1769488
  564.3 3.5 fusion.69
  567.8 5.7 all-reduce.2
  573.6 21.7 %all-reduce.3 = bf16[8,24,1]{1,0,2:T(8,128)(2,1)S(1)} all-reduce(f32[8,24,1]{1,0,2:T(8,128)S(1)} %dynamic-slice_convert_fusion), channel_id=3, replica_groups=mesh['dp'=8,'seq'=4] {'dp'}, use_global_device_ids=true, to_apply=%region_17.18.clone | all-reduce | flops 192 | bytes 1152
  596.2 5.6 all-reduce.1
  603.4 21.1 %reduce-scatter.19.cloned.1.call-done = f32[1,24,768]{2,1,0:T(8,128)} async-done(((f32[8,24,768]{2,1,0:T(8,128)}), f32[1,24,768]{2,1,0:T(8,128)}) %reduce-scatter.19.cloned.1.call-update) | async-done | bytes 73744 | tf_op jit(solution)/shard_map/reduce_scatter | solution.py:290
  625.3 5.5 all_gather.41
  631.5 59.9 %reduce-scatter.25.cloned.1.call-done = bf16[1,96,768]{2,1,0:T(8,128)(2,1)} async-done(((bf16[8,96,768]{2,1,0:T(8,128)(2,1)}), bf16[1,96,768]{2,1,0:T(8,128)(2,1)}) %reduce-scatter.25.cloned.1.call-update) | async-done | bytes 147472 | tf_op jit(solution)/shard_map/reduce_scatter | solution.py:292
  691.4 7.7 all_gather.43
  700.2 63.0 %reduce-scatter.21.cloned.1.call-done = f32[1,24,3072]{2,1,0:T(8,128)} async-done(((f32[8,24,3072]{2,1,0:T(8,128)}), f32[1,24,3072]{2,1,0:T(8,128)}) %reduce-scatter.21.cloned.1.call-update) | async-done | bytes 294928 | tf_op jit(solution)/shard_map/reduce_scatter | solution.py:291
  764.2 7.5 all_gather.42
  772.8 72.6 %reduce-scatter.17.cloned.1.call-done = f32[1,24,4608]{2,1,0:T(8,128)} async-done(((f32[8,24,4608]{2,1,0:T(8,128)}), f32[1,24,4608]{2,1,0:T(8,128)}) %reduce-scatter.17.cloned.1.call-update) | async-done | bytes 442384 | tf_op jit(solution)/shard_map/reduce_scatter | solution.py:289
  846.5 9.1 %all_gather.40 = bf16[1,96,4608]{2,1,0:T(8,128)(2,1)S(1)} all-gather(bf16[1,24,4608]{2,1,0:T(8,128)(2,1)S(1)} %convert_element_type.256), channel_id=1, replica_groups=mesh['dp'=8,'seq'=4] {'seq'}, dimensions={1}, use_global_device_ids=true | all-gather | bytes 1105920 | tf_op jit(solution)/shard_map/all_gather | solution.py:298
  (226 shorter events, 102.6 us)
Async XLA Ops:
  7.2 71.1 %all-gather.6.cloned.1.call-start = ((), (), s32[]{:S(2)}) async-start(), calls=%async_computation.12 | async-start | bytes 3981312 | tf_op jit(solution)/shard_map/all_gather | solution.py:96
  7.9 136.3 %all-gather.10.cloned.1.call-start = ((), (), s32[]{:S(2)}) async-start(), calls=%async_computation.14 | async-start | bytes 3981312 | tf_op jit(solution)/shard_map/all_gather | solution.py:100
  8.6 177.3 %all-gather.8.cloned.1.call-start = ((), (), s32[]{:S(2)}) async-start(), calls=%async_computation.13 | async-start | bytes 1327104 | tf_op jit(solution)/shard_map/all_gather | solution.py:97
  9.4 257.3 %all-gather.12.cloned.1.call-start = ((), (), s32[]{:S(2)}) async-start(), calls=%async_computation.15 | async-start | bytes 5308416 | tf_op jit(solution)/shard_map/all_gather | solution.py:101
  36.1 46.0 %copy-start.13 = (f32[768]{0:T(1024)}, f32[768]{0:T(1024)S(1)}, u32[]{:S(2)}) copy-start(f32[768]{0:T(1024)S(1)} %convert_element_type.231) | copy-start | bytes 9220
  37.2 44.8 %copy-start.16 = (f32[256]{0:T(256)}, f32[256]{0:T(256)S(1)}, u32[]{:S(2)}) copy-start(f32[256]{0:T(256)S(1)} %broadcast_multiply_fusion.6) | copy-start | bytes 3076
  38.5 43.6 %copy-start.18 = (f32[256]{0:T(256)}, f32[256]{0:T(256)S(1)}, u32[]{:S(2)}) copy-start(f32[256]{0:T(256)S(1)} %add_rsqrt_fusion.1) | copy-start | bytes 3076
  39.3 42.9 %copy-start.11 = (f32[256,32]{0,1:T(8,128)}, f32[256,32]{0,1:T(8,128)S(1)}, u32[]{:S(2)}) copy-start(f32[256,32]{0,1:T(8,128)S(1)} %get-tuple-element.453) | copy-start | bytes 98308
  82.7 6.6 copy-start.24
  83.8 19.4 %all-to-all-start = ((bf16[256,3,4,192]{0,3,1,2:T(8,128)(2,1)}), bf16[256,3,4,192]{0,3,1,2:T(8,128)(2,1)S(1)}, u32[]{:S(2)}, u32[]{:S(2)}) async-start(bf16[256,3,4,192]{0,3,1,2:T(8,128)(2,1)} %copy.70), calls=%async_computation | async-start | bytes 2359296 | tf_op jit(solution)/shard_map/all_to_all | solution.py:122
  87.4 259.4 %all-gather.14.cloned.1.call-start = ((), (), s32[]{:S(2)}) async-start(), calls=%async_computation.16 | async-start | bytes 5308416 | tf_op jit(solution)/shard_map/all_gather | solution.py:102
  132.4 14.4 %copy-start.28 = (s32[2]{0:T(128)}, s32[2]{0:T(128)S(1)}, u32[]{:S(2)}) copy-start(s32[2]{0:T(128)S(1)} %get-tuple-element.735) | copy-start | bytes 28
  132.8 53.2 %copy-start.3 = (bf16[256,768]{1,0:T(8,128)(2,1)S(1)}, bf16[256,768]{1,0:T(8,128)(2,1)}, u32[]{:S(2)}) copy-start(bf16[256,768]{1,0:T(8,128)(2,1)} %param.14) | copy-start | bytes 1179652
  133.8 52.2 %all-to-all-start.1 = ((bf16[4,256,192]{1,2,0:T(8,128)(2,1)}), bf16[4,256,192]{1,2,0:T(8,128)(2,1)S(1)}, u32[]{:S(2)}, u32[]{:S(2)}) async-start(bf16[4,256,192]{1,2,0:T(8,128)(2,1)} %copy.74), calls=%async_computation.1 | async-start | bytes 786432 | tf_op jit(solution)/shard_map/all_to_all | solution.py:157
  137.2 357.6 %reduce-scatter.29.cloned.1.call-start = ((), (), s32[]{:S(2)}) async-start(), calls=%async_computation.23 | async-start | bytes 1474560
  266.7 80.1 %copy-start.27 = (bf16[256,768]{1,0:T(8,128)(2,1)S(1)}, bf16[256,768]{1,0:T(8,128)(2,1)}, u32[]{:S(2)}) copy-start(bf16[256,768]{1,0:T(8,128)(2,1)} %param.21) | copy-start | bytes 1179652
  346.8 6.8 copy-start.25
  353.5 2.2 copy-start.8
  353.6 2.9 copy-start.26
  353.6 3.9 copy-start.30
  360.9 8.1 copy-start.5
  362.5 134.3 %reduce-scatter.23.cloned.1.call-start = ((), (), s32[]{:S(2)}) async-start(), calls=%async_computation.20 | async-start | bytes 5898240 | tf_op jit(solution)/shard_map/reduce_scatter | solution.py:280
  368.9 1.3 copy-start.7
  371.7 14.7 %all-to-all-start.2 = ((bf16[256,4,192]{0,2,1:T(8,128)(2,1)}), bf16[256,4,192]{0,2,1:T(8,128)(2,1)S(1)}, u32[]{:S(2)}, u32[]{:S(2)}) async-start(bf16[256,4,192]{0,2,1:T(8,128)(2,1)} %bitcast.16), calls=%async_computation.2 | async-start | bytes 786432 | tf_op jit(solution)/shard_map/all_to_all | solution.py:192
  375.1 122.4 %reduce-scatter.31.cloned.1.call-start = ((), (), s32[]{:S(2)}) async-start(), calls=%async_computation.24 | async-start | bytes 5898240
  381.0 6.8 copy-start.29
  389.7 9.3 %copy-start = (f32[3,512,1024]{2,1,0:T(8,128)}, f32[3,512,1024]{2,1,0:T(8,128)S(1)}, u32[]{:S(2)}) copy-start(f32[3,512,1024]{2,1,0:T(8,128)S(1)} %fusion.153) | copy-start | bytes 18874372 | tf_op jit(solution)/shard_map/while
  395.2 3.8 copy-start.2
  400.8 3.3 copy-start.1
  404.2 4.0 copy-start.9
  412.0 9.3 %copy-start = (f32[3,512,1024]{2,1,0:T(8,128)}, f32[3,512,1024]{2,1,0:T(8,128)S(1)}, u32[]{:S(2)}) copy-start(f32[3,512,1024]{2,1,0:T(8,128)S(1)} %fusion.153) | copy-start | bytes 18874372 | tf_op jit(solution)/shard_map/while
  417.5 3.8 copy-start.2
  423.1 3.5 copy-start.1
  426.6 4.3 copy-start.9
  436.9 6.4 copy-start.21
  436.9 6.4 copy-start.22
  436.9 6.4 copy-start.23
  436.9 6.5 copy-start.20
  439.5 37.0 %all-to-all-start.3 = ((bf16[1024,3,1,192]{3,1,2,0:T(4,128)(2,1)}), bf16[1024,3,1,192]{3,1,2,0:T(4,128)(2,1)S(1)}, u32[]{:S(2)}, u32[]{:S(2)}) async-start(bf16[1024,3,1,192]{3,1,2,0:T(4,128)(2,1)} %copy.80), calls=%async_computation.3 | async-start | bytes 4194304 | tf_op jit(solution)/shard_map/all_to_all | solution.py:234
  443.1 115.4 %reduce-scatter.27.cloned.1.call-start = ((), (), s32[]{:S(2)}) async-start(), calls=%async_computation.22 | async-start | bytes 8847360
  480.3 1.0 copy-start.14
  480.3 1.0 copy-start.17
  480.3 1.0 copy-start.19
  494.8 129.7 %reduce-scatter.19.cloned.1.call-start = ((), (), s32[]{:S(2)}) async-start(), calls=%async_computation.18 | async-start | bytes 663552 | tf_op jit(solution)/shard_map/reduce_scatter | solution.py:290
  496.8 194.6 %reduce-scatter.25.cloned.1.call-start = ((), (), s32[]{:S(2)}) async-start(), calls=%async_computation.21 | async-start | bytes 1327104 | tf_op jit(solution)/shard_map/reduce_scatter | solution.py:292
  497.5 265.7 %reduce-scatter.21.cloned.1.call-start = ((), (), s32[]{:S(2)}) async-start(), calls=%async_computation.19 | async-start | bytes 2654208 | tf_op jit(solution)/shard_map/reduce_scatter | solution.py:291
  501.7 343.8 %reduce-scatter.17.cloned.1.call-start = ((), (), s32[]{:S(2)}) async-start(), calls=%async_computation.17 | async-start | bytes 3981312 | tf_op jit(solution)/shard_map/reduce_scatter | solution.py:289
  564.2 38.1 %copy-start.6 = (f32[256,768]{1,0:T(8,128)S(1)}, f32[256,768]{1,0:T(8,128)}, u32[]{:S(2)}) copy-start(f32[256,768]{1,0:T(8,128)} %copy-done.5) | copy-start | bytes 2359300
  (5 other events, 4.1 us)
Sparse Core Ops, SparseCore 0:
  10.2 68.0 all-gather.5
  80.5 63.6 all-gather.9
  146.4 39.5 all-gather.7
  188.0 78.6 all-gather.11
  268.7 78.0 all-gather.13
  362.6 27.1 reduce-scatter.28
  392.6 45.1 reduce-scatter.22
  440.3 55.2 reduce-scatter.30
  498.2 60.2 reduce-scatter.26
  562.2 62.1 reduce-scatter.18
  628.2 63.1 reduce-scatter.24
  695.2 67.9 reduce-scatter.20
  767.3 78.1 reduce-scatter.16
where the time goes:
time: 873 us; the launch traced here: 864 us
  waiting for transfers between devices  565 us (65%)
  blocking collectives  86 us (10%)
  matrix products  79.7 us (9%)
  other arithmetic  53.6 us (6%)
  local copies, waits for them, and re-layouts  46.8 us (5%)
  between operations  17.3 us (2%)
  starting transfers between devices  15.4 us (2%)
    all_gather x1, waiting for transfers between devices, body(): lax.all_gather(w_up, 'dp', axis=0, tiled=True)  78.6 us
    all_gather x1, waiting for transfers between devices, body(): lax.all_gather(w_down, 'dp', axis=0, tiled=True)  74.6 us
    reduce_scatter x1, waiting for transfers between devices, body(): lax.psum_scatter(parts[1], 'dp', scatter_dimension=0, tiled=True)  72.6 us
    reduce_scatter x1, waiting for transfers between devices, body(): lax.psum_scatter(parts[3], 'dp', scatter_dimension=0, tiled=True)  63 us
    unnamed x16, waiting for transfers between devices  60.7 us
    reduce_scatter x1, waiting for transfers between devices, body(): lax.psum_scatter(parts[4], 'dp', scatter_dimension=0, tiled=True)  59.9 us
    unnamed x4, blocking collectives  56.3 us
    all_gather x1, waiting for transfers between devices, body(): lax.all_gather(w_out, 'dp', axis=0, tiled=True)  39.1 us
  transfers between devices with their start and end apart: 17, of which 13 were waited for; matrix products, arithmetic and copies ran while one was open for 18% of the time, Pallas kernels for 0%

commit v1 on v0

--- a/solution.py
+++ b/solution.py
@@ -8,6 +8,19 @@
 HEAD_DIM = 64
 eps = 1e-05
 neg_fill = -1e30
+
+
+def ring_gather(x, axis, dim):
+    ways = lax.axis_size(axis)
+    up = [(d, (d + 1) % ways) for d in range(ways)]
+    down = [(d, (d - 1) % ways) for d in range(ways)]
+    earlier, later = ([x], [x])
+    for _ in range(ways // 2):
+        earlier.append(lax.ppermute(earlier[-1], axis, up))
+    for _ in range((ways - 1) // 2):
+        later.append(lax.ppermute(later[-1], axis, down))
+    line = jnp.concatenate([*earlier[::-1], *later[1:]], axis=dim)
+    return jnp.roll(line, (lax.axis_index(axis) - ways // 2) * x.shape[dim], axis=dim)
 
 
 def layer_norm(values_in):
@@ -99,7 +112,7 @@
     ada_weight, up_weight, down_weight = (
         lax.all_gather(w_ada, "dp", axis=0, tiled=True),
         lax.all_gather(w_up, "dp", axis=0, tiled=True),
-        lax.all_gather(w_down, "dp", axis=0, tiled=True),
+        ring_gather(w_down, "dp", 0),
     )
     gain_float = gain_full.astype(jnp.float32)
     inputs = tokens.astype(jnp.float32)

time: 873 us -> 846 us (0.969)
  waiting for transfers between devices: 565 us -> 489 us
  local copies, waits for them, and re-layouts: 46.8 us -> 63.6 us
  blocking collectives: 86 us -> 101 us
  starting transfers between devices: 15.4 us -> 28.7 us
    all_gather x1 -> x0, waiting for transfers between devices: 74.6 us -> none  [body(): lax.all_gather(w_down, 'dp', axis=0, tiled=True)]
    ppermute x0 -> x7, waiting for transfers between devices: none -> 60.8 us  [the longest x4 42 us: ring_gather(): earlier.append(lax.ppermute(earlier[-1], axis, up))]
    all_gather x1, waiting for transfers between devices: 39 us -> 0.01 us  [body(): lax.all_gather(w_qkv, 'dp', axis=0, tiled=True)]
    unnamed x66 -> x99, local copies, waits for them, and re-layouts: 24 us -> 39 us
    unnamed x4, blocking collectives: 56.3 us -> 70.9 us
    ppermute x0 -> x7, starting transfers between devices: none -> 13.5 us  [the longest x4 7.76 us: ring_gather(): earlier.append(lax.ppermute(earlier[-1], axis, up))]
    all_gather x1, waiting for transfers between devices: 39.1 us -> 29.8 us  [body(): lax.all_gather(w_out, 'dp', axis=0, tiled=True)]
    unnamed x16 -> x15, waiting for transfers between devices: 60.7 us -> 59.1 us
  transfers between devices with their start and end apart: 17 -> 23, of which waited for: 13 -> 15; matrix products, arithmetic and copies ran while one was open for 18% -> 20% of each run, Pallas kernels for 0% -> 0%
where the time goes in v1:
time: 846 us; the launch traced here: 836 us
  waiting for transfers between devices  489 us (58%)
  blocking collectives  101 us (12%)
  matrix products  81.4 us (10%)
  local copies, waits for them, and re-layouts  63.6 us (8%)
  other arithmetic  54.3 us (6%)
  starting transfers between devices  28.7 us (3%)
  between operations  18 us (2%)
    all_gather x1, waiting for transfers between devices, body(): lax.all_gather(w_up, 'dp', axis=0, tiled=True)  78.6 us
    reduce_scatter x1, waiting for transfers between devices, body(): lax.psum_scatter(parts[1], 'dp', scatter_dimension=0, tiled=True)  72.6 us
    unnamed x4, blocking collectives  70.9 us
    reduce_scatter x1, waiting for transfers between devices, body(): lax.psum_scatter(parts[3], 'dp', scatter_dimension=0, tiled=True)  63.3 us
    reduce_scatter x1, waiting for transfers between devices, body(): lax.psum_scatter(parts[4], 'dp', scatter_dimension=0, tiled=True)  59.7 us
    unnamed x15, waiting for transfers between devices  59.1 us
    ppermute x4, waiting for transfers between devices, ring_gather(): earlier.append(lax.ppermute(earlier[-1], axis, up))  42 us
    unnamed x99, local copies, waits for them, and re-layouts  39 us
  transfers between devices with their start and end apart: 23, of which 15 were waited for; matrix products, arithmetic and copies ran while one was open for 20% of the time, Pallas kernels for 0%

profile of v1, /device:TPU:0, one launch (start us, length us, event | category | flops | bytes accessed | tf_op | source)
XLA Modules:
  0.0 835.7 jit_solution(13166399848430753878)
XLA Ops:
  9.4 3.0 collective-permute-start
  12.5 19.8 %collective-permute-done = bf16[384,768]{1,0:T(8,128)(2,1)S(1)} collective-permute-done((bf16[384,768]{1,0:T(8,128)(2,1)}, bf16[384,768]{1,0:T(8,128)(2,1)S(1)}, u32[]{:S(2)}, u32[]{:S(2)}) %collective-permute-start) | collective-permute-done | bytes 589856 | tf_op jit(solution)/shard_map/ppermute | solution.py:19
  32.5 4.5 collective-permute-start.4
  38.9 21.7 %collective-permute-done.1 = bf16[384,768]{1,0:T(8,128)(2,1)S(1)} collective-permute-done((bf16[384,768]{1,0:T(8,128)(2,1)S(1)}, bf16[384,768]{1,0:T(8,128)(2,1)S(1)}, u32[]{:S(2)}, u32[]{:S(2)}) %collective-permute-start.1) | collective-permute-done | bytes 589856 | tf_op jit(solution)/shard_map/ppermute | solution.py:19
  66.0 37.7 %all-reduce = bf16[768]{0:T(1024)(128)(2,1)S(1)} all-reduce(bf16[768]{0:T(1024)(128)(2,1)S(1)} %dynamic-update-slice), channel_id=1, replica_groups=mesh['dp'=8,'seq'=4] {'dp'}, use_global_device_ids=true, to_apply=%add | all-reduce | flops 768 | bytes 3072
  110.5 15.6 %collective-permute-done.5 = bf16[384,768]{1,0:T(8,128)(2,1)S(1)} collective-permute-done((bf16[384,768]{1,0:T(8,128)(2,1)S(1)}, bf16[384,768]{1,0:T(8,128)(2,1)S(1)}, u32[]{:S(2)}, u32[]{:S(2)}) %collective-permute-start.5) | collective-permute-done | bytes 589856 | tf_op jit(solution)/shard_map/ppermute | solution.py:21
  133.8 3.2 collective-permute-done.6
  139.6 3.6 fusion.90
  145.6 3.5 all-to-all-start
  157.5 7.5 all-to-all-done
  168.7 25.4 %while.30 = (s32[]{:T(128)}, bf16[2,512,3,64]{1,3,2,0:T(8,128)(2,1)S(1)}, f32[2,3,512]{2,1,0:T(4,128)}, s32[]{:T(128)}, s32[2]{0:T(128)S(1)}, /*index=5*/s32[]{:...) while((s32[]{:T(128)}, ...), condition=%wide.region_5.6_spmd.clone.clone, body=%wide.region_2.5_spmd.clone.clone.sunk | while | flops 422682112 | bytes 22220956 | solution.py:169
  177.5 3.2 fusion.145
  190.2 3.2 fusion.145
  195.4 3.5 all-to-all-start.1
  201.7 29.8 %all-gather.7.cloned.1.call-done = bf16[768,768]{1,0:T(8,128)(2,1)} async-done(((bf16[96,768]{1,0:T(8,128)(2,1)}), bf16[768,768]{1,0:T(8,128)(2,1)}) %all-gather.7.cloned.1.call-update) | async-done | bytes 1179664 | tf_op jit(solution)/shard_map/all_gather | solution.py:110
  233.6 78.6 %all-gather.11.cloned.1.call-done = bf16[768,3072]{1,0:T(8,128)(2,1)} async-done(((bf16[96,3072]{1,0:T(8,128)(2,1)}), bf16[768,3072]{1,0:T(8,128)(2,1)}) %all-gather.11.cloned.1.call-update) | async-done | bytes 4718608 | tf_op jit(solution)/shard_map/all_gather | solution.py:114
  312.3 3.9 fusion.92
  316.2 7.2 fusion.60
  325.7 6.3 fusion.78
  333.6 6.4 convolution_convert_fusion
  342.8 3.5 all-to-all-start.2
  346.5 3.0 convolution_convert_fusion.1
  352.1 5.5 all-to-all-done.2
  359.0 45.2 %while.31 = (s32[]{:T(128)}, f32[1024,3,64]{0,2,1:T(8,128)}, f32[1024,3,64]{0,2,1:T(8,128)}, bf16[2,512,3,64]{1,3,2,0:T(8,128)(2,1)}, bf16[2,512,3,64]{1,3,2,0:T...) while((s32[]{:T(128)}, f32[1024,3,64]{0,2,1:T(8,128)}, ...), condition=%wide.region_12.13_spmd.clone.clone, body=%wide.region_10.12_spmd.clone.clone.sunk | while | flops 1032363520 | bytes 110420320 | solution.py:239
  366.6 3.8 multiply_reduce_fusion.7
  372.2 2.6 fusion.156
  375.4 4.0 fusion.157
  388.9 3.8 multiply_reduce_fusion.7
  394.5 2.9 fusion.156
  398.0 4.3 fusion.157
  411.0 3.6 all-to-all-start.3
  417.3 31.1 %all-to-all-done.3 = bf16[1024,3,1,192]{3,1,2,0:T(4,128)(2,1)S(1)} async-done(((bf16[1024,3,1,192]{3,1,2,0:T(4,128)(2,1)}), bf16[1024,3,1,192]{3,1,2,0:T(4,128)(2,1)S(1)}, u32[]{:S(2)}, u32[]{:S(2)}) %all-to-all-start.3) | async-done | bytes 1179680 | tf_op jit(solution)/shard_map/all_to_all | solution.py:247
  448.4 2.8 copy.84
  454.5 5.4 pad_maximum_fusion
  459.9 6.7 copy.95
  473.5 56.3 %reduce-scatter.27.cloned.1.call-done = bf16[24,36864]{1,0:T(8,128)(2,1)} async-done(((bf16[96,36864]{1,0:T(8,128)(2,1)}), bf16[24,36864]{1,0:T(8,128)(2,1)}) %reduce-scatter.27.cloned.1.call-update) | async-done | bytes 1769488
  535.5 3.5 fusion.75
  539.1 5.7 all-reduce.2
  544.9 21.8 %all-reduce.3 = bf16[8,24,1]{1,0,2:T(8,128)(2,1)S(1)} all-reduce(f32[8,24,1]{1,0,2:T(8,128)S(1)} %dynamic-slice_convert_fusion), channel_id=3, replica_groups=mesh['dp'=8,'seq'=4] {'dp'}, use_global_device_ids=true, to_apply=%region_17.18.clone | all-reduce | flops 192 | bytes 1152
  567.6 5.6 all-reduce.1
  574.9 21.0 %reduce-scatter.19.cloned.1.call-done = f32[1,24,768]{2,1,0:T(8,128)} async-done(((f32[8,24,768]{2,1,0:T(8,128)}), f32[1,24,768]{2,1,0:T(8,128)}) %reduce-scatter.19.cloned.1.call-update) | async-done | bytes 73744 | tf_op jit(solution)/shard_map/reduce_scatter | solution.py:303
  596.7 5.5 all_gather.37
  602.9 59.7 %reduce-scatter.25.cloned.1.call-done = bf16[1,96,768]{2,1,0:T(8,128)(2,1)} async-done(((bf16[8,96,768]{2,1,0:T(8,128)(2,1)}), bf16[1,96,768]{2,1,0:T(8,128)(2,1)}) %reduce-scatter.25.cloned.1.call-update) | async-done | bytes 147472 | tf_op jit(solution)/shard_map/reduce_scatter | solution.py:305
  662.6 7.7 all_gather.39
  671.4 63.3 %reduce-scatter.21.cloned.1.call-done = f32[1,24,3072]{2,1,0:T(8,128)} async-done(((f32[8,24,3072]{2,1,0:T(8,128)}), f32[1,24,3072]{2,1,0:T(8,128)}) %reduce-scatter.21.cloned.1.call-update) | async-done | bytes 294928 | tf_op jit(solution)/shard_map/reduce_scatter | solution.py:304
  735.7 7.5 all_gather.38
  744.2 72.6 %reduce-scatter.17.cloned.1.call-done = f32[1,24,4608]{2,1,0:T(8,128)} async-done(((f32[8,24,4608]{2,1,0:T(8,128)}), f32[1,24,4608]{2,1,0:T(8,128)}) %reduce-scatter.17.cloned.1.call-update) | async-done | bytes 442384 | tf_op jit(solution)/shard_map/reduce_scatter | solution.py:302
  817.9 9.1 %all_gather.36 = bf16[1,96,4608]{2,1,0:T(8,128)(2,1)S(1)} all-gather(bf16[1,24,4608]{2,1,0:T(8,128)(2,1)S(1)} %convert_element_type.256), channel_id=1, replica_groups=mesh['dp'=8,'seq'=4] {'seq'}, dimensions={1}, use_global_device_ids=true | all-gather | bytes 1105920 | tf_op jit(solution)/shard_map/all_gather | solution.py:311
  (272 shorter events, 133.0 us)
Async XLA Ops:
  7.2 132.4 %all-gather.5.cloned.1.call-start = ((), (), s32[]{:S(2)}) async-start(), calls=%async_computation.12 | async-start | bytes 3981312 | tf_op jit(solution)/shard_map/all_gather | solution.py:109
  7.9 191.2 %all-gather.9.cloned.1.call-start = ((), (), s32[]{:S(2)}) async-start(), calls=%async_computation.14 | async-start | bytes 3981312 | tf_op jit(solution)/shard_map/all_gather | solution.py:113
  8.7 222.9 %all-gather.7.cloned.1.call-start = ((), (), s32[]{:S(2)}) async-start(), calls=%async_computation.13 | async-start | bytes 1327104 | tf_op jit(solution)/shard_map/all_gather | solution.py:110
  9.4 121.8 %copy-start.8 = (bf16[384,768]{1,0:T(8,128)(2,1)S(1)}, bf16[384,768]{1,0:T(8,128)(2,1)}, u32[]{:S(2)}) copy-start(bf16[384,768]{1,0:T(8,128)(2,1)} %param.20) | copy-start | bytes 1769476
  9.4 302.9 %all-gather.11.cloned.1.call-start = ((), (), s32[]{:S(2)}) async-start(), calls=%async_computation.15 | async-start | bytes 5308416 | tf_op jit(solution)/shard_map/all_gather | solution.py:114
  9.4 22.8 %collective-permute-start = (bf16[384,768]{1,0:T(8,128)(2,1)}, bf16[384,768]{1,0:T(8,128)(2,1)S(1)}, u32[]{:S(2)}, u32[]{:S(2)}) collective-permute-start(bf16[384,768]{1,0:T(8,128)(2,1)} %param.20), channel_id=1, source_target_pairs={{0,4},{4,8},{8,12},{12,16},{16,20},{20,24},{24,28},{28,0},{1,5},{5... | collective-permute-start | bytes 1769480 | tf_op jit(solution)/shard_map/ppermute | solution.py:19
  32.2 28.4 %collective-permute-start.1 = (bf16[384,768]{1,0:T(8,128)(2,1)S(1)}, bf16[384,768]{1,0:T(8,128)(2,1)S(1)}, u32[]{:S(2)}, u32[]{:S(2)}) collective-permute-start(bf16[384,768]{1,0:T(8,128)(2,1)S(1)} %collective-permute-done), channel_id=1, source_target_pairs={{0,4},{4,8},{8,12},{12,16},{16,20},{20,24},{24,28},{28,0},{1,5},{5... | collective-permute-start | bytes 1769480 | tf_op jit(solution)/shard_map/ppermute | solution.py:19
  32.5 73.8 %collective-permute-start.4 = (bf16[384,768]{1,0:T(8,128)(2,1)}, bf16[384,768]{1,0:T(8,128)(2,1)S(1)}, u32[]{:S(2)}, u32[]{:S(2)}) collective-permute-start(bf16[384,768]{1,0:T(8,128)(2,1)} %param.20), channel_id=1, source_target_pairs={{0,28},{4,0},{8,4},{12,8},{16,12},{20,16},{24,20},{28,24},{1,29},{... | collective-permute-start | bytes 1769480 | tf_op jit(solution)/shard_map/ppermute | solution.py:21
  60.6 71.5 %copy-start.11 = (bf16[384,768]{1,0:T(8,128)(2,1)}, bf16[384,768]{1,0:T(8,128)(2,1)S(1)}, u32[]{:S(2)}) copy-start(bf16[384,768]{1,0:T(8,128)(2,1)S(1)} %collective-permute-done.1) | copy-start | bytes 1769476
  60.6 45.8 %collective-permute-start.2 = (bf16[384,768]{1,0:T(8,128)(2,1)S(1)}, bf16[384,768]{1,0:T(8,128)(2,1)S(1)}, u32[]{:S(2)}, u32[]{:S(2)}) collective-permute-start(bf16[384,768]{1,0:T(8,128)(2,1)S(1)} %collective-permute-done.1), channel_id=1, source_target_pairs={{0,4},{4,8},{8,12},{12,16},{16,20},{20,24},{24,28},{28,0},{1,5},{5... | collective-permute-start | bytes 1769480 | tf_op jit(solution)/shard_map/ppermute | solution.py:19
  103.7 35.9 %copy-start.22 = (f32[768]{0:T(1024)}, f32[768]{0:T(1024)S(1)}, u32[]{:S(2)}) copy-start(f32[768]{0:T(1024)S(1)} %convert_element_type.231) | copy-start | bytes 9220
  106.2 33.4 %copy-start.26 = (f32[256]{0:T(256)}, f32[256]{0:T(256)S(1)}, u32[]{:S(2)}) copy-start(f32[256]{0:T(256)S(1)} %broadcast_multiply_fusion.6) | copy-start | bytes 3076
  106.3 25.8 %copy-start.9 = (bf16[384,768]{1,0:T(8,128)(2,1)}, bf16[384,768]{1,0:T(8,128)(2,1)S(1)}, u32[]{:S(2)}) copy-start(bf16[384,768]{1,0:T(8,128)(2,1)S(1)} %collective-permute-done.4) | copy-start | bytes 1769476
  106.3 19.8 %collective-permute-start.5 = (bf16[384,768]{1,0:T(8,128)(2,1)S(1)}, bf16[384,768]{1,0:T(8,128)(2,1)S(1)}, u32[]{:S(2)}, u32[]{:S(2)}) collective-permute-start(bf16[384,768]{1,0:T(8,128)(2,1)S(1)} %collective-permute-done.4), channel_id=1, source_target_pairs={{0,28},{4,0},{8,4},{12,8},{16,12},{20,16},{24,20},{28,24},{1,29},{... | collective-permute-start | bytes 1769480 | tf_op jit(solution)/shard_map/ppermute | solution.py:21
  106.4 24.0 %copy-start.12 = (bf16[384,768]{1,0:T(8,128)(2,1)}, bf16[384,768]{1,0:T(8,128)(2,1)S(1)}, u32[]{:S(2)}) copy-start(bf16[384,768]{1,0:T(8,128)(2,1)S(1)} %collective-permute-done.2) | copy-start | bytes 1769476
  106.4 21.4 %collective-permute-start.3 = (bf16[384,768]{1,0:T(8,128)(2,1)S(1)}, bf16[384,768]{1,0:T(8,128)(2,1)S(1)}, u32[]{:S(2)}, u32[]{:S(2)}) collective-permute-start(bf16[384,768]{1,0:T(8,128)(2,1)S(1)} %collective-permute-done.2), channel_id=1, source_target_pairs={{0,4},{4,8},{8,12},{12,16},{16,20},{20,24},{24,28},{28,0},{1,5},{5... | collective-permute-start | bytes 1769480 | tf_op jit(solution)/shard_map/ppermute | solution.py:19
  109.6 30.0 %copy-start.28 = (f32[256]{0:T(256)}, f32[256]{0:T(256)S(1)}, u32[]{:S(2)}) copy-start(f32[256]{0:T(256)S(1)} %add_rsqrt_fusion.1) | copy-start | bytes 3076
  126.0 6.9 copy-start.13
  126.0 11.0 %collective-permute-start.6 = (bf16[384,768]{1,0:T(8,128)(2,1)S(1)}, bf16[384,768]{1,0:T(8,128)(2,1)S(1)}, u32[]{:S(2)}, u32[]{:S(2)}) collective-permute-start(bf16[384,768]{1,0:T(8,128)(2,1)S(1)} %collective-permute-done.5), channel_id=1, source_target_pairs={{0,28},{4,0},{8,4},{12,8},{16,12},{20,16},{24,20},{28,24},{1,29},{... | collective-permute-start | bytes 1769480 | tf_op jit(solution)/shard_map/ppermute | solution.py:21
  131.2 8.4 %copy-start.3 = (bf16[256,768]{1,0:T(8,128)(2,1)S(1)}, bf16[256,768]{1,0:T(8,128)(2,1)}, u32[]{:S(2)}) copy-start(bf16[256,768]{1,0:T(8,128)(2,1)} %param.14) | copy-start | bytes 1179652
  145.6 19.4 %all-to-all-start = ((bf16[256,3,4,192]{0,3,1,2:T(8,128)(2,1)}), bf16[256,3,4,192]{0,3,1,2:T(8,128)(2,1)S(1)}, u32[]{:S(2)}, u32[]{:S(2)}) async-start(bf16[256,3,4,192]{0,3,1,2:T(8,128)(2,1)} %copy.70), calls=%async_computation | async-start | bytes 2359296 | tf_op jit(solution)/shard_map/all_to_all | solution.py:135
  149.1 5.7 copy-start.10
  149.1 6.6 copy-start.14
  151.2 5.4 copy-start.16
  195.4 36.1 %all-to-all-start.1 = ((bf16[4,256,192]{1,2,0:T(8,128)(2,1)}), bf16[4,256,192]{1,2,0:T(8,128)(2,1)S(1)}, u32[]{:S(2)}, u32[]{:S(2)}) async-start(bf16[4,256,192]{1,2,0:T(8,128)(2,1)} %copy.74), calls=%async_computation.1 | async-start | bytes 786432 | tf_op jit(solution)/shard_map/all_to_all | solution.py:170
  198.9 267.8 %reduce-scatter.29.cloned.1.call-start = ((), (), s32[]{:S(2)}) async-start(), calls=%async_computation.22 | async-start | bytes 1474560
  312.3 11.2 %slice-start = ((s8[4718592]{0:T(1024)(128)(4,1)}), s8[4194304]{0:T(1024)(128)(4,1)S(1)}, s32[]{:S(2)}) async-start(s8[4718592]{0:T(1024)(128)(4,1)} %bitcast.245), calls=%async_computation.24 | async-start | bytes 8388608
  316.2 9.5 %copy-start.37 = (f32[256,3072]{1,0:T(8,128)}, f32[256,3072]{1,0:T(8,128)S(1)}, u32[]{:S(2)}) copy-start(f32[256,3072]{1,0:T(8,128)S(1)} %fusion.92) | copy-start | bytes 9437188
  316.2 7.2 slice-start.1
  332.0 8.2 copy-start.5
  333.6 135.1 %reduce-scatter.23.cloned.1.call-start = ((), (), s32[]{:S(2)}) async-start(), calls=%async_computation.19 | async-start | bytes 5898240 | tf_op jit(solution)/shard_map/reduce_scatter | solution.py:293
  342.8 14.8 %all-to-all-start.2 = ((bf16[256,4,192]{0,2,1:T(8,128)(2,1)}), bf16[256,4,192]{0,2,1:T(8,128)(2,1)S(1)}, u32[]{:S(2)}, u32[]{:S(2)}) async-start(bf16[256,4,192]{0,2,1:T(8,128)(2,1)} %bitcast.16), calls=%async_computation.2 | async-start | bytes 786432 | tf_op jit(solution)/shard_map/all_to_all | solution.py:205
  346.3 123.1 %reduce-scatter.31.cloned.1.call-start = ((), (), s32[]{:S(2)}) async-start(), calls=%async_computation.23 | async-start | bytes 5898240
  352.1 6.9 copy-start.36
  360.9 9.4 %copy-start = (f32[3,512,1024]{2,1,0:T(8,128)}, f32[3,512,1024]{2,1,0:T(8,128)S(1)}, u32[]{:S(2)}) copy-start(f32[3,512,1024]{2,1,0:T(8,128)S(1)} %fusion.155) | copy-start | bytes 18874372 | tf_op jit(solution)/shard_map/while
  383.3 9.4 %copy-start = (f32[3,512,1024]{2,1,0:T(8,128)}, f32[3,512,1024]{2,1,0:T(8,128)S(1)}, u32[]{:S(2)}) copy-start(f32[3,512,1024]{2,1,0:T(8,128)S(1)} %fusion.155) | copy-start | bytes 18874372 | tf_op jit(solution)/shard_map/while
  398.0 4.3 copy-start.18
  408.4 6.5 copy-start.31
  408.4 6.5 copy-start.32
  408.4 6.5 copy-start.33
  408.4 6.5 copy-start.30
  411.0 37.5 %all-to-all-start.3 = ((bf16[1024,3,1,192]{3,1,2,0:T(4,128)(2,1)}), bf16[1024,3,1,192]{3,1,2,0:T(4,128)(2,1)S(1)}, u32[]{:S(2)}, u32[]{:S(2)}) async-start(bf16[1024,3,1,192]{3,1,2,0:T(4,128)(2,1)} %copy.80), calls=%async_computation.3 | async-start | bytes 4194304 | tf_op jit(solution)/shard_map/all_to_all | solution.py:247
  414.6 115.2 %reduce-scatter.27.cloned.1.call-start = ((), (), s32[]{:S(2)}) async-start(), calls=%async_computation.21 | async-start | bytes 8847360
  466.7 129.2 %reduce-scatter.19.cloned.1.call-start = ((), (), s32[]{:S(2)}) async-start(), calls=%async_computation.17 | async-start | bytes 663552 | tf_op jit(solution)/shard_map/reduce_scatter | solution.py:303
  468.7 193.9 %reduce-scatter.25.cloned.1.call-start = ((), (), s32[]{:S(2)}) async-start(), calls=%async_computation.20 | async-start | bytes 1327104 | tf_op jit(solution)/shard_map/reduce_scatter | solution.py:305
  469.2 265.4 %reduce-scatter.21.cloned.1.call-start = ((), (), s32[]{:S(2)}) async-start(), calls=%async_computation.18 | async-start | bytes 2654208 | tf_op jit(solution)/shard_map/reduce_scatter | solution.py:304
  473.4 343.4 %reduce-scatter.17.cloned.1.call-start = ((), (), s32[]{:S(2)}) async-start(), calls=%async_computation.16 | async-start | bytes 3981312 | tf_op jit(solution)/shard_map/reduce_scatter | solution.py:302
  535.5 38.3 %copy-start.6 = (f32[256,768]{1,0:T(8,128)S(1)}, f32[256,768]{1,0:T(8,128)}, u32[]{:S(2)}) copy-start(f32[256,768]{1,0:T(8,128)} %copy-done.5) | copy-start | bytes 2359300
  (20 other events, 38.0 us)
Sparse Core Ops, SparseCore 0:
  10.2 97.6 all-gather.4
  110.1 79.6 all-gather.8
  191.9 39.5 all-gather.6
  233.6 78.6 all-gather.10
  333.7 27.2 reduce-scatter.28
  363.6 45.1 reduce-scatter.22
  411.3 55.6 reduce-scatter.30
  469.7 60.0 reduce-scatter.26
  533.7 62.0 reduce-scatter.18
  599.4 63.1 reduce-scatter.24
  666.5 68.1 reduce-scatter.20
  738.6 78.2 reduce-scatter.16
